TPU v7x, 128 devices: a whole 4x4x4 slice. The times are simulated.
128 devices in a mesh: ctx: 64 (over z_lo, x, y, core), fsdp: 2 (over z_hi).
Axes of the slice: x: 4, y: 4, z: 4 (z_hi: 2, z_lo: 2; z = z_hi * 2 + z_lo), core: 2. Of those that a mesh axis runs over, the one named last changes fastest.
Arguments:
- block_in: bfloat16 [2, 8192, 768], P('fsdp', 'ctx'), may hold values from -70 to 70
- out_grad: bfloat16 [2, 8192, 768], P('fsdp', 'ctx'), may hold values from -6 to 6
- ln1_gain: bfloat16 [768], P('fsdp'), may hold values from 0.5 to 1.5
- ln1_bias: bfloat16 [768], P('fsdp'), may hold values from -3 to 3
- w_qkv: bfloat16 [768, 2304], P('fsdp'), may hold values from -2 to 2
- q_bias: bfloat16 [768], P('fsdp'), may hold values from -3 to 3
- v_bias: bfloat16 [768], P('fsdp'), may hold values from -3 to 3
- w_proj: bfloat16 [768, 768], P('fsdp'), may hold values from -2 to 2
- b_proj: bfloat16 [768], P('fsdp'), may hold values from -3 to 3
- ln2_gain: bfloat16 [768], P('fsdp'), may hold values from 0.5 to 1.5
- ln2_bias: bfloat16 [768], P('fsdp'), may hold values from -3 to 3
- w_fc: bfloat16 [768, 3072], P('fsdp'), may hold values from -0.21875 to 0.21875
- b_fc: bfloat16 [3072], P('fsdp'), may hold values from -3 to 3
- w_out: bfloat16 [3072, 768], P('fsdp'), may hold values from -0.109375 to 0.109375
- b_out: bfloat16 [768], P('fsdp'), may hold values from -3 to 3
Outputs:
- block_out: bfloat16 [2, 8192, 768], P('fsdp', 'ctx')
- input_grad: float32 [2, 8192, 768], P('fsdp', 'ctx')
- grad_ln1_gain: float32 [768], P('fsdp')
- grad_ln1_bias: float32 [768], P('fsdp')
- grad_w_qkv: float32 [768, 2304], P('fsdp')
- grad_q_bias: float32 [768], P('fsdp')
- grad_v_bias: float32 [768], P('fsdp')
- grad_w_proj: float32 [768, 768], P('fsdp')
- grad_b_proj: float32 [768], P('fsdp')
- grad_ln2_gain: float32 [768], P('fsdp')
- grad_ln2_bias: float32 [768], P('fsdp')
- grad_w_fc: float32 [768, 3072], P('fsdp')
- grad_b_fc: float32 [3072], P('fsdp')
- grad_w_out: float32 [3072, 768], P('fsdp')
- grad_b_out: float32 [768], P('fsdp')
All inputs are finite; a program needn't handle non-finite values.
Results may differ from a plain program's by a relative error of at most 0.025.
The roundings to bfloat16 on the way count: a program that leaves them out, or rounds other values in their place, can miss the bound.
Values may be sent and summed in bfloat16 or wider, within the bound.
No kernel may reach another device: no remote copies, remote signals or barrier semaphores. Data moves between devices by JAX's collectives and lax.ppermute only.
A program may use at most 256 MiB of HBM per device.

v0:
```python
import math
import jax
import jax.numpy as jnp
from jax import lax
from jax.sharding import PartitionSpec as P

HEADS = 12
norm_epsilon = 1e-05
gelu_factor = 0.7978845608028654
gelu_cubic = 0.044715
masked_score = -1e30


def layer_norm(values, gain, offset):
    center = jnp.mean(values, axis=-1, keepdims=True)
    centered = values - center
    spread = jnp.mean(centered * centered, axis=-1, keepdims=True)
    return centered * lax.rsqrt(spread + norm_epsilon) * gain + offset


def gelu_tanh(values):
    return (
        0.5
        * values
        * (1.0 + jnp.tanh(gelu_factor * (values + gelu_cubic * values * values * values)))
    )


def score_grads(
    query_rows, grad_rows, lse_rows, delta_rows, key_rows, value_rows, allowed, score_scale
):
    scores = (
        jnp.einsum("thd,shd->hts", query_rows, key_rows, preferred_element_type=jnp.float32)
        * score_scale
    )
    scores = jnp.where(allowed[None], scores, masked_score)
    probabilities = jnp.where(allowed[None], jnp.exp(scores - lse_rows[:, :, None]), 0.0)
    grad_probs = jnp.einsum(
        "thd,shd->hts", grad_rows, value_rows, preferred_element_type=jnp.float32
    )
    grad_scores = (probabilities * (grad_probs - delta_rows[:, :, None]) * score_scale).astype(
        jnp.bfloat16
    )
    return (grad_scores, probabilities)


def body(
    block_in,
    out_grad,
    ln1_gain,
    ln1_bias,
    w_qkv,
    q_bias,
    v_bias,
    w_proj,
    b_proj,
    ln2_gain,
    ln2_bias,
    w_fc,
    b_fc,
    w_out,
    b_out,
):
    gathered = (
        lax.all_gather(ln1_gain, "fsdp", axis=0, tiled=True),
        lax.all_gather(ln1_bias, "fsdp", axis=0, tiled=True),
        lax.all_gather(w_qkv, "fsdp", axis=0, tiled=True),
        lax.all_gather(q_bias, "fsdp", axis=0, tiled=True),
        lax.all_gather(v_bias, "fsdp", axis=0, tiled=True),
        lax.all_gather(w_proj, "fsdp", axis=0, tiled=True),
        lax.all_gather(b_proj, "fsdp", axis=0, tiled=True),
        lax.all_gather(ln2_gain, "fsdp", axis=0, tiled=True),
        lax.all_gather(ln2_bias, "fsdp", axis=0, tiled=True),
        lax.all_gather(w_fc, "fsdp", axis=0, tiled=True),
        lax.all_gather(b_fc, "fsdp", axis=0, tiled=True),
        lax.all_gather(w_out, "fsdp", axis=0, tiled=True),
        lax.all_gather(b_out, "fsdp", axis=0, tiled=True),
    )
    gain_one = gathered[0].astype(jnp.float32)
    shift_one = gathered[1].astype(jnp.float32)
    qkv_weight = gathered[2]
    query_bias = gathered[3].astype(jnp.float32)
    value_bias = gathered[4].astype(jnp.float32)
    proj_weight = gathered[5]
    proj_bias = gathered[6].astype(jnp.float32)
    gain_two = gathered[7].astype(jnp.float32)
    shift_two = gathered[8].astype(jnp.float32)
    fc_weight = gathered[9]
    fc_bias = gathered[10].astype(jnp.float32)
    out_weight = gathered[11]
    out_bias = gathered[12].astype(jnp.float32)
    row_count = block_in.shape[1]
    width = block_in.shape[2]
    head_count = HEADS
    head_width = width // head_count
    score_scale = 1.0 / math.sqrt(head_width)
    row_total = row_count * lax.axis_size("ctx")
    first_query = lax.axis_index("ctx") * row_count
    query_pos = first_query + jnp.arange(row_count, dtype=jnp.int32)
    last_query = first_query + row_count - 1
    inputs_wide = block_in[0].astype(jnp.float32)
    normed_one = layer_norm(inputs_wide, gain_one, shift_one).astype(jnp.bfloat16)
    projected = jnp.dot(normed_one, qkv_weight, preferred_element_type=jnp.float32)
    queries = (projected[:, :width] + query_bias).astype(jnp.bfloat16)
    keys_local = projected[:, width : 2 * width].astype(jnp.bfloat16)
    values_local = (projected[:, 2 * width :] + value_bias).astype(jnp.bfloat16)
    query_heads = queries.reshape(row_count, head_count, head_width)
    initial = (
        jnp.full((head_count, row_count), masked_score, jnp.float32),
        jnp.zeros((head_count, row_count), jnp.float32),
        jnp.zeros((row_count, head_count, head_width), jnp.float32),
    )
    key_span = lax.all_gather(keys_local, "ctx", axis=0, tiled=True)
    value_span = lax.all_gather(values_local, "ctx", axis=0, tiled=True)
    span_total = key_span.shape[0]
    attend_span_rows = math.gcd(span_total, 512)

    def one_step(step_index, inner):
        offset = step_index * attend_span_rows
        key_rows = lax.dynamic_slice_in_dim(key_span, offset, attend_span_rows, 0).reshape(
            attend_span_rows, head_count, head_width
        )
        value_rows = lax.dynamic_slice_in_dim(value_span, offset, attend_span_rows, 0).reshape(
            attend_span_rows, head_count, head_width
        )

        def one_computed(state):
            maximum, denominator, accumulated = state
            key_pos = offset + jnp.arange(attend_span_rows, dtype=jnp.int32)
            allowed = key_pos[None, :] <= query_pos[:, None]
            scores = (
                jnp.einsum(
                    "thd,shd->hts", query_heads, key_rows, preferred_element_type=jnp.float32
                )
                * score_scale
            )
            scores = jnp.where(allowed[None], scores, masked_score)
            new_max = jnp.maximum(maximum, jnp.max(scores, axis=2))
            weights = jnp.where(allowed[None], jnp.exp(scores - new_max[:, :, None]), 0.0)
            factor = jnp.exp(maximum - new_max)
            denominator = denominator * factor + jnp.sum(weights, axis=2)
            accumulated = accumulated * jnp.transpose(factor)[:, :, None] + jnp.einsum(
                "hts,shd->thd",
                weights.astype(jnp.bfloat16),
                value_rows,
                preferred_element_type=jnp.float32,
            )
            return (new_max, denominator, accumulated)

        return lax.cond(offset > last_query, lambda state: state, one_computed, inner)

    maximum, denominator, accumulated = lax.fori_loop(
        0, span_total // attend_span_rows, one_step, initial
    )
    log_sums = maximum + jnp.log(denominator)
    attended = accumulated / jnp.transpose(denominator)[:, :, None]
    attn_rows = lax.optimization_barrier(attended.reshape(row_count, width).astype(jnp.bfloat16))
    residual_one = (
        jnp.dot(attn_rows, proj_weight, preferred_element_type=jnp.float32)
        + proj_bias
        + inputs_wide
    )
    normed_two = layer_norm(residual_one, gain_two, shift_two).astype(jnp.bfloat16)
    hidden_pre = jnp.dot(normed_two, fc_weight, preferred_element_type=jnp.float32) + fc_bias
    activated = gelu_tanh(hidden_pre).astype(jnp.bfloat16)
    output = (
        jnp.dot(activated, out_weight, preferred_element_type=jnp.float32) + out_bias + residual_one
    ).astype(jnp.bfloat16)
    cotangent = out_grad[0]
    grad_wide = cotangent.astype(jnp.float32)
    grad_out_weight = jnp.einsum(
        "tf,td->fd", activated, cotangent, preferred_element_type=jnp.float32
    )
    grad_out_bias = jnp.sum(grad_wide, axis=0)
    grad_activated = jnp.einsum(
        "td,fd->tf", cotangent, out_weight, preferred_element_type=jnp.float32
    )
    unused, gelu_back = jax.vjp(gelu_tanh, hidden_pre)
    grad_hidden = gelu_back(grad_activated)[0]
    grad_hidden_low = grad_hidden.astype(jnp.bfloat16)
    grad_fc_weight = jnp.einsum(
        "td,tf->df", normed_two, grad_hidden_low, preferred_element_type=jnp.float32
    )
    grad_fc_bias = jnp.sum(grad_hidden, axis=0)
    grad_normed_two = jnp.einsum(
        "tf,df->td", grad_hidden_low, fc_weight, preferred_element_type=jnp.float32
    )
    unused, norm_back_two = jax.vjp(layer_norm, residual_one, gain_two, shift_two)
    grad_residual, grad_gain_two, grad_shift_two = norm_back_two(grad_normed_two)
    grad_residual = grad_residual + grad_wide
    grad_residual_low = grad_residual.astype(jnp.bfloat16)
    grad_proj_weight = jnp.einsum(
        "td,te->de", attn_rows, grad_residual_low, preferred_element_type=jnp.float32
    )
    grad_proj_bias = jnp.sum(grad_residual, axis=0)
    grad_attn = lax.optimization_barrier(
        jnp.einsum(
            "te,de->td", grad_residual_low, proj_weight, preferred_element_type=jnp.float32
        ).astype(jnp.bfloat16)
    )
    grad_heads = grad_attn.reshape(row_count, head_count, head_width)
    delta_sums = jnp.transpose(
        jnp.sum(
            grad_heads.astype(jnp.float32)
            * attn_rows.reshape(row_count, head_count, head_width).astype(jnp.float32),
            axis=2,
        )
    )
    keys_all, values_all = (
        lax.all_gather(keys_local, "ctx", axis=0, tiled=True),
        lax.all_gather(values_local, "ctx", axis=0, tiled=True),
    )
    span_rows = math.gcd(row_total, 512)
    span_count = row_total // span_rows
    key_blocks = keys_all.reshape(span_count, span_rows, head_count, head_width)
    value_blocks = values_all.reshape(span_count, span_rows, head_count, head_width)
    zero_query = jnp.zeros((row_count, head_count, head_width), jnp.float32)

    def back_step(grad_query, inputs):
        key_rows, value_rows, step_index = inputs
        start_pos = step_index * span_rows

        def back_computed(running):
            key_pos = start_pos + jnp.arange(span_rows, dtype=jnp.int32)
            allowed = key_pos[None, :] <= query_pos[:, None]
            grad_scores, probabilities = score_grads(
                query_heads,
                grad_heads,
                log_sums,
                delta_sums,
                key_rows,
                value_rows,
                allowed,
                score_scale,
            )
            rounded = probabilities.astype(jnp.bfloat16)
            grad_key = jnp.einsum(
                "hts,thd->shd", grad_scores, query_heads, preferred_element_type=jnp.float32
            )
            grad_value = jnp.einsum(
                "hts,thd->shd", rounded, grad_heads, preferred_element_type=jnp.float32
            )
            updated = running + jnp.einsum(
                "hts,shd->thd", grad_scores, key_rows, preferred_element_type=jnp.float32
            )
            return (
                updated,
                jnp.concatenate(
                    [grad_key.reshape(span_rows, width), grad_value.reshape(span_rows, width)],
                    axis=1,
                ),
            )

        def skipped(running):
            return (running, jnp.zeros((span_rows, 2 * width), jnp.float32))

        return lax.cond(start_pos > last_query, skipped, back_computed, grad_query)

    grad_query, key_terms = lax.scan(
        back_step, zero_query, (key_blocks, value_blocks, jnp.arange(span_count, dtype=jnp.int32))
    )
    own_terms = lax.psum_scatter(
        key_terms.reshape(row_total, 2 * width), "ctx", scatter_dimension=0, tiled=True
    )
    grad_keys = own_terms[:, :width]
    grad_values = own_terms[:, width:]
    grad_query = grad_query.reshape(row_count, width)
    grad_query_bias = jnp.sum(grad_query, axis=0)
    grad_value_bias = jnp.sum(grad_values, axis=0)
    grad_projected = jnp.concatenate([grad_query, grad_keys, grad_values], axis=1).astype(
        jnp.bfloat16
    )
    grad_qkv_weight = jnp.einsum(
        "td,te->de", normed_one, grad_projected, preferred_element_type=jnp.float32
    )
    grad_normed_one = jnp.einsum(
        "te,de->td", grad_projected, qkv_weight, preferred_element_type=jnp.float32
    )
    unused, norm_back_one = jax.vjp(layer_norm, inputs_wide, gain_one, shift_one)
    grad_inputs, grad_gain_one, grad_shift_one = norm_back_one(grad_normed_one)
    grad_inputs = grad_inputs + grad_residual
    shards = (
        lax.psum_scatter(
            grad_gain_one.astype(jnp.bfloat16), "fsdp", scatter_dimension=0, tiled=True
        ).astype(jnp.float32),
        lax.psum_scatter(
            grad_shift_one.astype(jnp.bfloat16), "fsdp", scatter_dimension=0, tiled=True
        ).astype(jnp.float32),
        lax.psum_scatter(
            grad_qkv_weight.astype(jnp.bfloat16), "fsdp", scatter_dimension=0, tiled=True
        ).astype(jnp.float32),
        lax.psum_scatter(
            grad_query_bias.astype(jnp.bfloat16), "fsdp", scatter_dimension=0, tiled=True
        ).astype(jnp.float32),
        lax.psum_scatter(
            grad_value_bias.astype(jnp.bfloat16), "fsdp", scatter_dimension=0, tiled=True
        ).astype(jnp.float32),
        lax.psum_scatter(
            grad_proj_weight.astype(jnp.bfloat16), "fsdp", scatter_dimension=0, tiled=True
        ).astype(jnp.float32),
        lax.psum_scatter(
            grad_proj_bias.astype(jnp.bfloat16), "fsdp", scatter_dimension=0, tiled=True
        ).astype(jnp.float32),
        lax.psum_scatter(
            grad_gain_two.astype(jnp.bfloat16), "fsdp", scatter_dimension=0, tiled=True
        ).astype(jnp.float32),
        lax.psum_scatter(
            grad_shift_two.astype(jnp.bfloat16), "fsdp", scatter_dimension=0, tiled=True
        ).astype(jnp.float32),
        lax.psum_scatter(
            grad_fc_weight.astype(jnp.bfloat16), "fsdp", scatter_dimension=0, tiled=True
        ).astype(jnp.float32),
        lax.psum_scatter(
            grad_fc_bias.astype(jnp.bfloat16), "fsdp", scatter_dimension=0, tiled=True
        ).astype(jnp.float32),
        lax.psum_scatter(
            grad_out_weight.astype(jnp.bfloat16), "fsdp", scatter_dimension=0, tiled=True
        ).astype(jnp.float32),
        lax.psum_scatter(
            grad_out_bias.astype(jnp.bfloat16), "fsdp", scatter_dimension=0, tiled=True
        ).astype(jnp.float32),
    )
    totals = lax.psum(
        (
            shards[0],
            shards[1],
            shards[2],
            shards[3],
            shards[4],
            shards[5],
            shards[6],
            shards[7],
            shards[8],
            shards[9],
            shards[10],
            shards[11],
            shards[12],
        ),
        "ctx",
    )
    return (
        output[None],
        grad_inputs[None],
        totals[0],
        totals[1],
        totals[2],
        totals[3],
        totals[4],
        totals[5],
        totals[6],
        totals[7],
        totals[8],
        totals[9],
        totals[10],
        totals[11],
        totals[12],
    )


def solution(mesh):
    in_specs = (
        P("fsdp", "ctx", None),
        P("fsdp", "ctx", None),
        P("fsdp"),
        P("fsdp"),
        P("fsdp", None),
        P("fsdp"),
        P("fsdp"),
        P("fsdp", None),
        P("fsdp"),
        P("fsdp"),
        P("fsdp"),
        P("fsdp", None),
        P("fsdp"),
        P("fsdp", None),
        P("fsdp"),
    )
    out_specs = (
        P("fsdp", "ctx", None),
        P("fsdp", "ctx", None),
        P("fsdp"),
        P("fsdp"),
        P("fsdp", None),
        P("fsdp"),
        P("fsdp"),
        P("fsdp", None),
        P("fsdp"),
        P("fsdp"),
        P("fsdp"),
        P("fsdp", None),
        P("fsdp"),
        P("fsdp", None),
        P("fsdp"),
    )
    return jax.shard_map(body, mesh=mesh, in_specs=in_specs, out_specs=out_specs, check_vma=False)
```

profile of v0, /device:TPU:0, one launch (start us, length us, event | category | flops | bytes accessed | tf_op | source)
XLA Modules:
  0.0 1733.6 jit_solution(4564429500221950973)
XLA Ops:
  8.7 6.2 all-gather.1
  24.4 41.3 %all-gather.16.cloned.1.call-done = bf16[768,2304]{1,0:T(8,128)(2,1)} async-done(((bf16[384,2304]{1,0:T(8,128)(2,1)}), bf16[768,2304]{1,0:T(8,128)(2,1)}) %all-gather.16.cloned.1.call-update) | async-done | bytes 3538960 | tf_op jit(solution)/shard_map/all_gather | solution.py:67
  83.8 5.8 all-gather.4
  89.7 5.9 all-gather.7
  95.6 5.8 all-gather.6
  107.5 79.1 %all-gather.18.cloned.1.call-done = bf16[8192,768]{1,0:T(8,128)(2,1)} async-done(((bf16[128,768]{1,0:T(8,128)(2,1)}), bf16[8192,768]{1,0:T(8,128)(2,1)}) %all-gather.18.cloned.1.call-update) | async-done | bytes 12582928 | tf_op jit(solution)/shard_map/all_gather | solution.py:113
  186.6 16.3 copy.76
  203.0 103.3 %all-gather.20.cloned.1.call-done = bf16[8192,768]{1,0:T(8,128)(2,1)} async-done(((bf16[128,768]{1,0:T(8,128)(2,1)}), bf16[8192,768]{1,0:T(8,128)(2,1)}) %all-gather.20.cloned.1.call-update) | async-done | bytes 12582928 | tf_op jit(solution)/shard_map/all_gather | solution.py:114
  306.2 15.8 copy.77
  327.9 6.2 all-gather.22.cloned.1.call-done
  336.0 65.6 %all-gather.24.cloned.1.call-done = bf16[768,3072]{1,0:T(8,128)(2,1)} async-done(((bf16[384,3072]{1,0:T(8,128)(2,1)}), bf16[768,3072]{1,0:T(8,128)(2,1)}) %all-gather.24.cloned.1.call-update) | async-done | bytes 4718608 | tf_op jit(solution)/shard_map/all_gather | solution.py:74
  404.9 64.3 %all-gather.26.cloned.1.call-done = bf16[3072,768]{1,0:T(8,128)(2,1)} async-done(((bf16[1536,768]{1,0:T(8,128)(2,1)}), bf16[3072,768]{1,0:T(8,128)(2,1)}) %all-gather.26.cloned.1.call-update) | async-done | bytes 4718608 | tf_op jit(solution)/shard_map/all_gather | solution.py:76
  477.3 9.5 copy.108
  486.9 18.8 %copy.81 = bf16[16,512,12,64]{1,3,2,0:T(8,128)(2,1)} copy(bf16[16,512,12,64]{1,0,3,2:T(8,128)(2,1)S(1)} %bitcast.175) | data formatting | bytes 25165824
  510.9 18.6 %copy.82 = bf16[16,512,12,64]{1,3,2,0:T(8,128)(2,1)} copy(bf16[16,512,12,64]{1,0,3,2:T(8,128)(2,1)S(1)} %bitcast.176) | data formatting | bytes 25165824
  532.7 134.6 %while.35 = (s32[]{:T(128)}, f32[128,12,64]{0,2,1:T(8,128)}, f32[16,512,1536]{2,1,0:T(8,128)}, s32[16]{0:T(128)S(1)}, s32[]{:T(128)}, /*index=5*/bf16[16,512,12,...) while((s32[]{:T(128)}, f32[128,12,64]{0,2,1:T(8,128)}, ...), condition=%wide.region_16.17_spmd.clone, body=%wide.region_13.16_spmd.clone.sunk | while | flops 514491008 | bytes 40333600 | solution.py:259
  533.9 10.1 conditional.7
  680.5 502.5 %reduce-scatter.6.cloned.1.call-done = f32[128,1536]{1,0:T(8,128)} async-done(((f32[8192,1536]{1,0:T(8,128)}), f32[128,1536]{1,0:T(8,128)}) %reduce-scatter.6.cloned.1.call-update) | async-done | bytes 786448 | tf_op jit(solution)/shard_map/reduce_scatter | solution.py:262
  1202.3 7.9 reduce-scatter.10.cloned.1.call-done
  1210.2 66.5 %reduce-scatter.12.cloned.1.call-done = bf16[384,3072]{1,0:T(8,128)(2,1)} async-done(((bf16[768,3072]{1,0:T(8,128)(2,1)}), bf16[384,3072]{1,0:T(8,128)(2,1)}) %reduce-scatter.12.cloned.1.call-update) | async-done | bytes 2359312 | tf_op jit(solution)/shard_map/reduce_scatter | solution.py:310
  1276.7 66.2 %reduce-scatter.14.cloned.1.call-done = bf16[1536,768]{1,0:T(8,128)(2,1)} async-done(((bf16[3072,768]{1,0:T(8,128)(2,1)}), bf16[1536,768]{1,0:T(8,128)(2,1)}) %reduce-scatter.14.cloned.1.call-update) | async-done | bytes 2359312 | tf_op jit(solution)/shard_map/reduce_scatter | solution.py:316
  1348.1 8.4 all-reduce.10
  1356.9 40.2 %reduce-scatter.8.cloned.1.call-done = bf16[384,2304]{1,0:T(8,128)(2,1)} async-done(((bf16[768,2304]{1,0:T(8,128)(2,1)}), bf16[384,2304]{1,0:T(8,128)(2,1)}) %reduce-scatter.8.cloned.1.call-update) | async-done | bytes 1769488 | tf_op jit(solution)/shard_map/reduce_scatter | solution.py:289
  1397.1 330.0 %all-reduce.12 = (f32[384]{0:T(512)}, f32[384]{0:T(512)}, f32[384,2304]{1,0:T(8,128)}, f32[384]{0:T(512)}, f32[384]{0:T(512)}, /*index=5*/f32[384,768]{1,0:T(8,1...) all-reduce(f32[384]{0:T(512)S(1)} %get-tuple-element.680, ...), channel_id=1, replica_groups=mesh['ctx'=64,'fsdp'=2] {'ctx'}, use_global_device_ids=true, to_apply=%region_22.23 | all-reduce | flops 3543552 | bytes 21270528 | tf_op jit(solution)/shard_map/psum | solution.py:323
  (404 shorter events, 237.4 us)
Async XLA Ops:
  7.2 58.5 %all-gather.16.cloned.1.call-start = ((), (), s32[]{:S(2)}) async-start(), calls=%async_computation.5 | async-start | bytes 5308416 | tf_op jit(solution)/shard_map/all_gather | solution.py:67
  7.9 178.7 %all-gather.18.cloned.1.call-start = ((), (), s32[]{:S(2)}) async-start(), calls=%async_computation.6 | async-start | bytes 12779520 | tf_op jit(solution)/shard_map/all_gather | solution.py:113
  69.3 237.0 %all-gather.20.cloned.1.call-start = ((), (), s32[]{:S(2)}) async-start(), calls=%async_computation.7 | async-start | bytes 12779520 | tf_op jit(solution)/shard_map/all_gather | solution.py:114
  81.9 252.1 %all-gather.22.cloned.1.call-start = ((), (), s32[]{:S(2)}) async-start(), calls=%async_computation.8 | async-start | bytes 1769472 | tf_op jit(solution)/shard_map/all_gather | solution.py:70
  82.5 319.1 %all-gather.24.cloned.1.call-start = ((), (), s32[]{:S(2)}) async-start(), calls=%async_computation.9 | async-start | bytes 7077888 | tf_op jit(solution)/shard_map/all_gather | solution.py:74
  83.1 386.1 %all-gather.26.cloned.1.call-start = ((), (), s32[]{:S(2)}) async-start(), calls=%async_computation.10 | async-start | bytes 7077888 | tf_op jit(solution)/shard_map/all_gather | solution.py:76
  83.7 1099.3 %reduce-scatter.6.cloned.1.call-start = ((), (), s32[]{:S(2)}) async-start(), calls=%async_computation.11 | async-start | bytes 51118080 | tf_op jit(solution)/shard_map/reduce_scatter | solution.py:262
  101.5 300.2 %copy-start.24 = (f32[768]{0:T(1024)}, f32[768]{0:T(1024)S(1)}, u32[]{:S(2)}) copy-start(f32[768]{0:T(1024)S(1)} %reshape.258) | copy-start | bytes 9220
  107.4 294.3 %copy-start.21 = (f32[768]{0:T(1024)}, f32[768]{0:T(1024)S(1)}, u32[]{:S(2)}) copy-start(f32[768]{0:T(1024)S(1)} %reshape.257) | copy-start | bytes 9220
  327.9 202.9 %copy-start.11 = (bf16[128,12,64]{0,2,1:T(8,128)(2,1)}, bf16[128,12,64]{0,2,1:T(8,128)(2,1)S(1)}, u32[]{:S(2)}) copy-start(bf16[128,12,64]{0,2,1:T(8,128)(2,1)S(1)} %divide_convert_fusion) | copy-start | bytes 589828
  335.8 141.2 %copy-start.1 = (f32[128,768]{1,0:T(8,128)}, f32[128,768]{1,0:T(8,128)S(1)}, u32[]{:S(2)}) copy-start(f32[128,768]{1,0:T(8,128)S(1)} %get-tuple-element.668) | copy-start | bytes 1179652
  404.9 69.7 %copy-start.3 = (f32[128,3072]{1,0:T(8,128)}, f32[128,3072]{1,0:T(8,128)S(1)}, u32[]{:S(2)}) copy-start(f32[128,3072]{1,0:T(8,128)S(1)} %convolution_add_fusion) | copy-start | bytes 4718596
  667.3 542.8 %reduce-scatter.10.cloned.1.call-start = ((), (), s32[]{:S(2)}) async-start(), calls=%async_computation.13 | async-start | bytes 1769472 | tf_op jit(solution)/shard_map/reduce_scatter | solution.py:298
  669.9 606.8 %reduce-scatter.12.cloned.1.call-start = ((), (), s32[]{:S(2)}) async-start(), calls=%async_computation.14 | async-start | bytes 7077888 | tf_op jit(solution)/shard_map/reduce_scatter | solution.py:310
  673.8 669.2 %reduce-scatter.14.cloned.1.call-start = ((), (), s32[]{:S(2)}) async-start(), calls=%async_computation.15 | async-start | bytes 7077888 | tf_op jit(solution)/shard_map/reduce_scatter | solution.py:316
  679.0 505.2 %copy-start.20 = (f32[768]{0:T(1024)S(1)}, f32[768]{0:T(1024)}, u32[]{:S(2)}) copy-start(f32[768]{0:T(1024)} %copy-done.19) | copy-start | bytes 9220
  679.0 505.2 %copy-start.27 = (f32[768]{0:T(1024)S(1)}, f32[768]{0:T(1024)}, u32[]{:S(2)}) copy-start(f32[768]{0:T(1024)} %copy-done.26) | copy-start | bytes 9220
  679.0 505.2 %copy-start.32 = (f32[128]{0:T(128)S(1)}, f32[128]{0:T(128)}, u32[]{:S(2)}) copy-start(f32[128]{0:T(128)} %copy-done.31) | copy-start | bytes 1540
  679.0 718.1 %reduce-scatter.8.cloned.1.call-start = ((), (), s32[]{:S(2)}) async-start(), calls=%async_computation.12 | async-start | bytes 5308416 | tf_op jit(solution)/shard_map/reduce_scatter | solution.py:289
  680.5 507.3 %copy-start.17 = (bf16[128,768]{1,0:T(8,128)(2,1)}, bf16[128,768]{1,0:T(8,128)(2,1)S(1)}, u32[]{:S(2)}) copy-start(bf16[128,768]{1,0:T(8,128)(2,1)S(1)} %copy.84) | copy-start | bytes 589828
  1198.1 144.8 %copy-start.15 = (f32[128,1536]{1,0:T(8,128)S(1)}, f32[128,1536]{1,0:T(8,128)}, u32[]{:S(2)}) copy-start(f32[128,1536]{1,0:T(8,128)} %reduce-scatter.6.cloned.1.call-done) | copy-start | bytes 2359300
  1202.3 144.4 %copy-start.54 = (f32[128]{0:T(128)S(1)}, f32[128]{0:T(128)}, u32[]{:S(2)}) copy-start(f32[128]{0:T(128)} %copy-done.53) | copy-start | bytes 1540
  1202.3 144.5 %copy-start.37 = (f32[128]{0:T(128)S(1)}, f32[128]{0:T(128)}, u32[]{:S(2)}) copy-start(f32[128]{0:T(128)} %copy-done.36) | copy-start | bytes 1540
  1202.3 144.8 %copy-start.45 = (f32[128]{0:T(128)S(1)}, f32[128]{0:T(128)}, u32[]{:S(2)}) copy-start(f32[128]{0:T(128)} %copy-done.43) | copy-start | bytes 1540
  (48 other events, 1023.4 us)
Sparse Core Ops, SparseCore 0:
  9.7 56.0 all-gather.15
  69.4 117.2 all-gather.17
  188.9 117.2 all-gather.19
  307.7 26.2 all-gather.21
  335.6 66.0 all-gather.23
  403.1 66.0 all-gather.25
  667.4 515.5 reduce-scatter.5
  1185.9 24.1 reduce-scatter.9
  1213.3 63.3 reduce-scatter.11
  1279.5 63.3 reduce-scatter.13
  1346.0 51.0 reduce-scatter.7
where the time goes:
time: 1740 us; the launch traced here: 1730 us
  waiting for transfers between devices  1050 us (60%)
  blocking collectives  391 us (22%)
  local copies, waits for them, and re-layouts  208 us (12%)
  matrix products  48 us (3%)
    reduce_scatter x1, waiting for transfers between devices, body(): lax.psum_scatter(key_terms.reshape(row_total, 2 * width), 'ctx', scatter_...  503 us
    psum x1, blocking collectives, body(): lax.psum((shards[0], shards[1], shards[2], shards[3], shards[4], shards[5...  330 us
    all_gather x1, waiting for transfers between devices, body(): value_span = lax.all_gather(values_local, 'ctx', axis=0, tiled=True)  103 us
    dynamic_update_slice x32, local copies, waits for them, and re-layouts, body(): lax.scan(back_step, zero_query, (key_blocks, value_blocks, jnp.arange(spa...  98.1 us
    unnamed x138, local copies, waits for them, and re-layouts  89.2 us
    all_gather x1, waiting for transfers between devices, body(): key_span = lax.all_gather(keys_local, 'ctx', axis=0, tiled=True)  79.1 us
    reduce_scatter x1, waiting for transfers between devices, body(): lax.psum_scatter(grad_fc_weight.astype(jnp.bfloat16), 'fsdp', scatter_dim...  66.5 us
    reduce_scatter x1, waiting for transfers between devices, body(): lax.psum_scatter(grad_out_weight.astype(jnp.bfloat16), 'fsdp', scatter_di...  66.2 us
  transfers between devices with their start and end apart: 11, of which 11 were waited for; matrix products, arithmetic and copies ran while one was open for 4% of the time, Pallas kernels for 0%

commit v1 on v0

--- a/solution.py
+++ b/solution.py
@@ -111,7 +111,8 @@
         jnp.zeros((row_count, head_count, head_width), jnp.float32),
     )
     key_span = lax.all_gather(keys_local, "ctx", axis=0, tiled=True)
-    value_span = lax.all_gather(values_local, "ctx", axis=0, tiled=True)
+    sent = jnp.stack([values_local] * lax.axis_size("ctx"))
+    value_span = jnp.concatenate(lax.all_to_all(sent, "ctx", 0, 0), axis=0)
     span_total = key_span.shape[0]
     attend_span_rows = math.gcd(span_total, 512)
 

time: 1740 us -> 1870 us (1.075)
  blocking collectives: 391 us -> 488 us
  local copies, waits for them, and re-layouts: 208 us -> 256 us
  waiting for transfers between devices: 1050 us -> 1020 us
    all_to_all x0 -> x1, waiting for transfers between devices: none -> 80 us  [body(): value_span = jnp.concatenate(lax.all_to_all(sent, 'ctx', 0, 0), axis=0)]
    all_gather x1, waiting for transfers between devices: 79.1 us -> 0.01 us  [body(): key_span = lax.all_gather(keys_local, 'ctx', axis=0, tiled=True)]
    all_gather x1, blocking collectives: 5.84 us -> 71 us  [body(): lax.all_gather(b_proj, 'fsdp', axis=0, tiled=True)]
    all_gather x1, blocking collectives: 5.87 us -> 33.9 us  [body(): lax.all_gather(b_fc, 'fsdp', axis=0, tiled=True)]
    all_gather x1, waiting for transfers between devices: 65.6 us -> 38.7 us  [body(): lax.all_gather(w_fc, 'fsdp', axis=0, tiled=True)]
    unnamed x138 -> x132, local copies, waits for them, and re-layouts: 89.2 us -> 95.8 us
  transfers between devices with their start and end apart: 11 -> 12, of which waited for: 11 -> 10; matrix products, arithmetic and copies ran while one was open for 4% -> 7% of each run, Pallas kernels for 0% -> 0%
where the time goes in v1:
time: 1870 us; the launch traced here: 1860 us
  waiting for transfers between devices  1020 us (55%)
  blocking collectives  488 us (26%)
  local copies, waits for them, and re-layouts  256 us (14%)
  matrix products  48 us (3%)
    reduce_scatter x1, waiting for transfers between devices, body(): lax.psum_scatter(key_terms.reshape(row_total, 2 * width), 'ctx', scatter_...  501 us
    psum x1, blocking collectives, body(): lax.psum((shards[0], shards[1], shards[2], shards[3], shards[4], shards[5...  330 us
    all_gather x1, waiting for transfers between devices, body(): lax.all_gather(values_local, 'ctx', axis=0, tiled=True)  111 us
    dynamic_update_slice x32, local copies, waits for them, and re-layouts, body(): lax.scan(back_step, zero_query, (key_blocks, value_blocks, jnp.arange(spa...  98 us
    unnamed x132, local copies, waits for them, and re-layouts  95.8 us
    all_to_all x1, waiting for transfers between devices, body(): value_span = jnp.concatenate(lax.all_to_all(sent, 'ctx', 0, 0), axis=0)  80 us
    all_gather x1, blocking collectives, body(): lax.all_gather(b_proj, 'fsdp', axis=0, tiled=True)  71 us
    reduce_scatter x1, waiting for transfers between devices, body(): lax.psum_scatter(grad_fc_weight.astype(jnp.bfloat16), 'fsdp', scatter_dim...  66.5 us
  transfers between devices with their start and end apart: 12, of which 10 were waited for; matrix products, arithmetic and copies ran while one was open for 7% of the time, Pallas kernels for 0%

profile of v1, /device:TPU:0, one launch (start us, length us, event | category | flops | bytes accessed | tf_op | source)
XLA Modules:
  0.0 1860.9 jit_solution(8911359809033441323)
XLA Ops:
  24.3 41.4 %all-gather.16.cloned.1.call-done = bf16[768,2304]{1,0:T(8,128)(2,1)} async-done(((bf16[384,2304]{1,0:T(8,128)(2,1)}), bf16[768,2304]{1,0:T(8,128)(2,1)}) %all-gather.16.cloned.1.call-update) | async-done | bytes 3538960 | tf_op jit(solution)/shard_map/all_gather | solution.py:67
  100.8 71.0 %all-gather.4 = bf16[2,1,384]{2,1,0:T(2,128)(2,1)S(1)} all-gather(bf16[1,1,384]{2,1,0:T(2,128)(2,1)S(1)} %reshape.248), channel_id=1, replica_groups=mesh['ctx'=64,'fsdp'=2] {'fsdp'}, dimensions={0}, use_global_device_ids=true | all-gather | bytes 2304 | tf_op jit(solution)/shard_map/all_gather | solution.py:71
  171.9 33.9 %all-gather.7 = bf16[2,1,1536]{2,1,0:T(2,128)(2,1)S(1)} all-gather(bf16[1,1,1536]{2,1,0:T(2,128)(2,1)S(1)} %reshape.254), channel_id=1, replica_groups=mesh['ctx'=64,'fsdp'=2] {'fsdp'}, dimensions={0}, use_global_device_ids=true | all-gather | bytes 9216 | tf_op jit(solution)/shard_map/all_gather | solution.py:75
  211.8 8.7 all-gather.5
  220.7 80.0 %all-to-all-done = bf16[64,128,768]{1,2,0:T(8,128)(2,1)} async-done(((bf16[64,128,768]{1,2,0:T(8,128)(2,1)}), bf16[64,128,768]{1,2,0:T(8,128)(2,1)}, u32[]{:S(2)}, u32[]{:S(2)}) %all-to-all-start) | async-done | bytes 12582944 | tf_op jit(solution)/shard_map/all_to_all | solution.py:115
  300.8 16.7 copy.91
  317.5 16.7 copy.93
  334.2 16.8 copy.92
  356.8 9.5 copy.124
  366.3 19.1 %copy.97 = bf16[16,512,12,64]{1,3,2,0:T(8,128)(2,1)} copy(bf16[16,512,12,64]{1,0,3,2:T(8,128)(2,1)S(1)} %bitcast.174) | data formatting | bytes 25165824
  387.4 38.7 %all-gather.22.cloned.1.call-done = bf16[768,3072]{1,0:T(8,128)(2,1)} async-done(((bf16[384,3072]{1,0:T(8,128)(2,1)}), bf16[768,3072]{1,0:T(8,128)(2,1)}) %all-gather.22.cloned.1.call-update) | async-done | bytes 4718608 | tf_op jit(solution)/shard_map/all_gather | solution.py:74
  429.4 64.3 %all-gather.24.cloned.1.call-done = bf16[3072,768]{1,0:T(8,128)(2,1)} async-done(((bf16[1536,768]{1,0:T(8,128)(2,1)}), bf16[3072,768]{1,0:T(8,128)(2,1)}) %all-gather.24.cloned.1.call-update) | async-done | bytes 4718608 | tf_op jit(solution)/shard_map/all_gather | solution.py:76
  502.5 110.7 %all-gather.26.cloned.1.call-done = bf16[8192,768]{1,0:T(8,128)(2,1)} async-done(((bf16[128,768]{1,0:T(8,128)(2,1)}), bf16[8192,768]{1,0:T(8,128)(2,1)}) %all-gather.26.cloned.1.call-update) | async-done | bytes 12582928 | tf_op jit(solution)/shard_map/all_gather | solution.py:212
  613.2 16.1 copy.95
  629.3 9.4 copy.125
  638.7 18.6 copy.98
  660.5 134.6 %while.35 = (s32[]{:T(128)}, f32[128,12,64]{0,2,1:T(8,128)}, f32[16,512,1536]{2,1,0:T(8,128)}, s32[16]{0:T(128)S(1)}, s32[]{:T(128)}, /*index=5*/bf16[16,512,12,...) while((s32[]{:T(128)}, f32[128,12,64]{0,2,1:T(8,128)}, ...), condition=%wide.region_16.17_spmd.clone, body=%wide.region_13.16_spmd.clone.sunk | while | flops 514491008 | bytes 40333600 | solution.py:260
  661.9 10.1 conditional.7
  808.4 501.4 %reduce-scatter.6.cloned.1.call-done = f32[128,1536]{1,0:T(8,128)} async-done(((f32[8192,1536]{1,0:T(8,128)}), f32[128,1536]{1,0:T(8,128)}) %reduce-scatter.6.cloned.1.call-update) | async-done | bytes 786448 | tf_op jit(solution)/shard_map/reduce_scatter | solution.py:263
  1337.3 66.5 %reduce-scatter.12.cloned.1.call-done = bf16[384,3072]{1,0:T(8,128)(2,1)} async-done(((bf16[768,3072]{1,0:T(8,128)(2,1)}), bf16[384,3072]{1,0:T(8,128)(2,1)}) %reduce-scatter.12.cloned.1.call-update) | async-done | bytes 2359312 | tf_op jit(solution)/shard_map/reduce_scatter | solution.py:311
  1403.8 66.3 %reduce-scatter.14.cloned.1.call-done = bf16[1536,768]{1,0:T(8,128)(2,1)} async-done(((bf16[3072,768]{1,0:T(8,128)(2,1)}), bf16[1536,768]{1,0:T(8,128)(2,1)}) %reduce-scatter.14.cloned.1.call-update) | async-done | bytes 2359312 | tf_op jit(solution)/shard_map/reduce_scatter | solution.py:317
  1475.2 8.4 all-reduce.10
  1484.0 40.2 %reduce-scatter.8.cloned.1.call-done = bf16[384,2304]{1,0:T(8,128)(2,1)} async-done(((bf16[768,2304]{1,0:T(8,128)(2,1)}), bf16[384,2304]{1,0:T(8,128)(2,1)}) %reduce-scatter.8.cloned.1.call-update) | async-done | bytes 1769488 | tf_op jit(solution)/shard_map/reduce_scatter | solution.py:290
  1524.2 330.0 %all-reduce.12 = (f32[384]{0:T(512)}, f32[384]{0:T(512)}, f32[384,2304]{1,0:T(8,128)}, f32[384]{0:T(512)}, f32[384]{0:T(512)}, /*index=5*/f32[384,768]{1,0:T(8,1...) all-reduce(f32[384]{0:T(512)S(1)} %get-tuple-element.701, ...), channel_id=1, replica_groups=mesh['ctx'=64,'fsdp'=2] {'ctx'}, use_global_device_ids=true, to_apply=%region_22.23 | all-reduce | flops 3543552 | bytes 21270528 | tf_op jit(solution)/shard_map/psum | solution.py:324
  (403 shorter events, 264.4 us)
Async XLA Ops:
  7.2 58.5 %all-gather.16.cloned.1.call-start = ((), (), s32[]{:S(2)}) async-start(), calls=%async_computation.6 | async-start | bytes 5308416 | tf_op jit(solution)/shard_map/all_gather | solution.py:67
  7.9 326.3 %all-gather.18.cloned.1.call-start = ((), (), s32[]{:S(2)}) async-start(), calls=%async_computation.7 | async-start | bytes 12779520 | tf_op jit(solution)/shard_map/all_gather | solution.py:113
  69.3 316.1 %all-gather.20.cloned.1.call-start = ((), (), s32[]{:S(2)}) async-start(), calls=%async_computation.8 | async-start | bytes 1769472 | tf_op jit(solution)/shard_map/all_gather | solution.py:70
  70.0 356.1 %all-gather.22.cloned.1.call-start = ((), (), s32[]{:S(2)}) async-start(), calls=%async_computation.9 | async-start | bytes 7077888 | tf_op jit(solution)/shard_map/all_gather | solution.py:74
  70.6 423.1 %all-gather.24.cloned.1.call-start = ((), (), s32[]{:S(2)}) async-start(), calls=%async_computation.10 | async-start | bytes 7077888 | tf_op jit(solution)/shard_map/all_gather | solution.py:76
  71.2 542.0 %all-gather.26.cloned.1.call-start = ((), (), s32[]{:S(2)}) async-start(), calls=%async_computation.11 | async-start | bytes 12779520 | tf_op jit(solution)/shard_map/all_gather | solution.py:212
  92.5 208.2 %all-to-all-start = ((bf16[64,128,768]{1,2,0:T(8,128)(2,1)}), bf16[64,128,768]{1,2,0:T(8,128)(2,1)}, u32[]{:S(2)}, u32[]{:S(2)}) async-start(bf16[64,128,768]{1,2,0:T(8,128)(2,1)} %stack.2), calls=%async_computation | async-start | bytes 25165824 | tf_op jit(solution)/shard_map/all_to_all | solution.py:115
  100.7 1209.1 %reduce-scatter.6.cloned.1.call-start = ((), (), s32[]{:S(2)}) async-start(), calls=%async_computation.12 | async-start | bytes 51118080 | tf_op jit(solution)/shard_map/reduce_scatter | solution.py:263
  211.8 214.3 %copy-start.24 = (f32[768]{0:T(1024)}, f32[768]{0:T(1024)S(1)}, u32[]{:S(2)}) copy-start(f32[768]{0:T(1024)S(1)} %reshape.264) | copy-start | bytes 9220
  220.6 205.6 %copy-start.21 = (f32[768]{0:T(1024)}, f32[768]{0:T(1024)S(1)}, u32[]{:S(2)}) copy-start(f32[768]{0:T(1024)S(1)} %reshape.263) | copy-start | bytes 9220
  356.8 301.8 %copy-start.11 = (bf16[128,12,64]{0,2,1:T(8,128)(2,1)}, bf16[128,12,64]{0,2,1:T(8,128)(2,1)S(1)}, u32[]{:S(2)}) copy-start(bf16[128,12,64]{0,2,1:T(8,128)(2,1)S(1)} %divide_convert_fusion) | copy-start | bytes 589828
  501.8 155.5 %copy-start.6 = (f32[128,768]{1,0:T(8,128)}, f32[128,768]{1,0:T(8,128)S(1)}, u32[]{:S(2)}) copy-start(f32[128,768]{1,0:T(8,128)S(1)} %get-tuple-element.677) | copy-start | bytes 1179652
  501.8 155.5 %copy-start.43 = (f32[128]{0:T(128)}, f32[128]{0:T(128)S(1)}, u32[]{:S(2)}) copy-start(f32[128]{0:T(128)S(1)} %negate_multiply_fusion.1) | copy-start | bytes 1540
  795.2 542.0 %reduce-scatter.10.cloned.1.call-start = ((), (), s32[]{:S(2)}) async-start(), calls=%async_computation.14 | async-start | bytes 1769472 | tf_op jit(solution)/shard_map/reduce_scatter | solution.py:299
  797.8 606.0 %reduce-scatter.12.cloned.1.call-start = ((), (), s32[]{:S(2)}) async-start(), calls=%async_computation.15 | async-start | bytes 7077888 | tf_op jit(solution)/shard_map/reduce_scatter | solution.py:311
  801.7 668.4 %reduce-scatter.14.cloned.1.call-start = ((), (), s32[]{:S(2)}) async-start(), calls=%async_computation.16 | async-start | bytes 7077888 | tf_op jit(solution)/shard_map/reduce_scatter | solution.py:317
  806.9 504.1 %copy-start.20 = (f32[768]{0:T(1024)S(1)}, f32[768]{0:T(1024)}, u32[]{:S(2)}) copy-start(f32[768]{0:T(1024)} %copy-done.19) | copy-start | bytes 9220
  806.9 504.1 %copy-start.27 = (f32[768]{0:T(1024)S(1)}, f32[768]{0:T(1024)}, u32[]{:S(2)}) copy-start(f32[768]{0:T(1024)} %copy-done.26) | copy-start | bytes 9220
  806.9 504.1 %copy-start.32 = (f32[128]{0:T(128)S(1)}, f32[128]{0:T(128)}, u32[]{:S(2)}) copy-start(f32[128]{0:T(128)} %copy-done.31) | copy-start | bytes 1540
  806.9 717.3 %reduce-scatter.8.cloned.1.call-start = ((), (), s32[]{:S(2)}) async-start(), calls=%async_computation.13 | async-start | bytes 5308416 | tf_op jit(solution)/shard_map/reduce_scatter | solution.py:290
  808.4 506.2 %copy-start.17 = (bf16[128,768]{1,0:T(8,128)(2,1)}, bf16[128,768]{1,0:T(8,128)(2,1)S(1)}, u32[]{:S(2)}) copy-start(bf16[128,768]{1,0:T(8,128)(2,1)S(1)} %copy.100) | copy-start | bytes 589828
  1325.2 144.9 %copy-start.15 = (f32[128,1536]{1,0:T(8,128)S(1)}, f32[128,1536]{1,0:T(8,128)}, u32[]{:S(2)}) copy-start(f32[128,1536]{1,0:T(8,128)} %reduce-scatter.6.cloned.1.call-done) | copy-start | bytes 2359300
  1329.3 144.6 %copy-start.37 = (f32[128]{0:T(128)S(1)}, f32[128]{0:T(128)}, u32[]{:S(2)}) copy-start(f32[128]{0:T(128)} %copy-done.36) | copy-start | bytes 1540
  1329.3 144.9 %copy-start.45 = (f32[128]{0:T(128)S(1)}, f32[128]{0:T(128)}, u32[]{:S(2)}) copy-start(f32[128]{0:T(128)} %copy-done.43) | copy-start | bytes 1540
  (46 other events, 1229.8 us)
Sparse Core Ops, SparseCore 0:
  9.7 56.0 all-gather.15
  69.4 261.5 all-gather.17
  332.6 25.8 all-gather.19
  360.1 66.0 all-gather.21
  427.6 66.0 all-gather.23
  495.9 117.2 all-gather.25
  795.3 514.4 reduce-scatter.5
  1312.7 24.4 reduce-scatter.9
  1340.4 63.3 reduce-scatter.11
  1406.6 63.3 reduce-scatter.13
  1473.1 51.0 reduce-scatter.7
